TPU v7x, 512 devices: a whole 4x8x8 slice. The times are simulated.
512 devices in a mesh: frame: 64 (over x, z_hi, y), row: 8 (over z_lo, core).
Axes of the slice: x: 4, y: 8, z: 8 (z_hi: 2, z_lo: 4; z = z_hi * 4 + z_lo), core: 2. Of those that a mesh axis runs over, the one named last changes fastest.
Arguments:
- latents: bfloat16 [256, 32, 32, 320], P('frame', 'row'), may hold values from -20 to 20
- ln_gain: bfloat16 [320], replicated, may hold values from 0.099609375 to 1.8984375
- q_weight: bfloat16 [320, 320], replicated, may hold values from -0.30078125 to 0.30078125
- k_weight: bfloat16 [320, 320], replicated, may hold values from -3 to 3
- v_weight: bfloat16 [320, 320], replicated, may hold values from -0.3125 to 0.3125
- o_weight: bfloat16 [320, 320], replicated, may hold values from -0.3125 to 0.3125
- gn_gain: bfloat16 [320], replicated, may hold values from 0.099609375 to 1.8984375
- conv_weight: bfloat16 [3, 3, 320, 320], replicated, may hold values from -0.109375 to 0.109375
- conv_bias: bfloat16 [320], replicated, may hold values from -3 to 3
Outputs:
- output: bfloat16 [256, 32, 32, 320], P('frame', 'row')
All inputs are finite; a program needn't handle non-finite values.
Results may differ from a plain program's by a relative error of at most 0.0085.
The roundings to bfloat16 on the way count: a program that leaves them out, or rounds other values in their place, can miss the bound.
Values may be sent and summed in bfloat16 or wider, within the bound.
A program may use at most 64 MiB of HBM per device.

v0:
```python
import math
import jax
import jax.numpy as jnp
from jax import lax
from jax.sharding import PartitionSpec as P

HEADS = 8
GROUPS = 32


def spread_2(value, axis, source):
    kept = jnp.where(lax.axis_index(axis) == source, value, 0).astype(value.dtype)
    return lax.psum(kept, axis)


def shifted(block, axis, distance):
    devices = range(lax.axis_size(axis))
    route = [(i - distance, i) for i in devices if i - distance in devices]
    return lax.ppermute(block, axis, route)


def with_halo(value, sides, width):
    for axis, dim in sides:
        size, length = (lax.axis_size(axis), value.shape[dim])
        up = [(i, (i + 1) % size) for i in range(size - 1)]
        down = [(j, i) for i, j in up]
        last = lax.slice_in_dim(value, length - width, length, axis=dim)
        leading = lax.slice_in_dim(value, 0, width, axis=dim)
        before = lax.ppermute(last, axis, up)
        after = lax.ppermute(leading, axis, down)
        value = jnp.concatenate([before, value, after], axis=dim)
    return value


def layer_normed(values, gain_vec):
    floated = values.astype(jnp.float32)
    centre = floated - jnp.mean(floated, axis=-1, keepdims=True)
    spread = jnp.mean(centre * centre, axis=-1, keepdims=True)
    return (centre * lax.rsqrt(spread + 1e-05) * gain_vec.astype(jnp.float32)).astype(jnp.bfloat16)


def attend_frames(queries, key_set, value_set, factor):
    lead_keys = key_set[0]
    lead_values = value_set[0]

    def single(operands):
        frame_queries, frame_keys, frame_values = operands
        all_keys = jnp.concatenate([lead_keys, frame_keys], axis=0)
        all_values = jnp.concatenate([lead_values, frame_values], axis=0)
        scores = (
            jnp.einsum("qhd,khd->hqk", frame_queries, all_keys, preferred_element_type=jnp.float32)
            * factor
        )
        highest = jnp.max(scores, axis=-1, keepdims=True)
        raised = jnp.exp(scores - highest)
        totals = jnp.sum(raised, axis=-1)
        summed = jnp.einsum(
            "hqk,khd->qhd",
            raised.astype(jnp.bfloat16),
            all_values,
            preferred_element_type=jnp.float32,
        )
        return (summed / jnp.transpose(totals)[:, :, None]).astype(jnp.bfloat16)

    return lax.map(single, (queries, key_set[1:], value_set[1:]))


def body(latents, ln_gain, q_weight, k_weight, v_weight, o_weight, gn_gain, conv_weight, conv_bias):
    frames, row_count, col_count, channels = latents.shape
    tok_shard = row_count * col_count
    head_dim = channels // HEADS
    factor = 1.0 / math.sqrt(head_dim)
    tokens = latents.reshape(frames * tok_shard, channels)
    kv_weight = jnp.concatenate([k_weight, v_weight], axis=1)
    normed = layer_normed(tokens, ln_gain)
    queries = jnp.dot(normed, q_weight, preferred_element_type=jnp.float32).astype(jnp.bfloat16)
    queries = queries.reshape(frames, tok_shard, channels)
    paired = jnp.dot(normed, kv_weight, preferred_element_type=jnp.float32).astype(jnp.bfloat16)
    paired = paired.reshape(frames, tok_shard, 2 * channels)
    leading = spread_2(paired[0], "frame", 0)
    earlier = shifted(paired[frames - 1], "frame", 1)
    earlier = jnp.where(lax.axis_index("frame") == 0, paired[0], earlier)
    stacked = jnp.concatenate([leading[None], earlier[None], paired[: frames - 1]], axis=0)
    sent_queries = queries.reshape(frames, tok_shard, 1, HEADS, head_dim)
    sent_pairs = stacked.reshape(frames + 1, tok_shard, 2, HEADS, head_dim)
    got_queries, got_pairs = (
        lax.all_to_all(sent_queries, "row", split_axis=3, concat_axis=1, tiled=True),
        lax.all_to_all(sent_pairs, "row", split_axis=3, concat_axis=1, tiled=True),
    )
    head_results = attend_frames(
        got_queries[:, :, 0], got_pairs[:, :, 0], got_pairs[:, :, 1], factor
    )
    returned = lax.all_to_all(head_results, "row", split_axis=1, concat_axis=2, tiled=True)
    attended = returned.reshape(frames * tok_shard, channels)
    mixed = jnp.dot(attended, o_weight, preferred_element_type=jnp.float32)
    updated = (tokens.astype(jnp.float32) + mixed).astype(jnp.bfloat16)
    group_width = channels // GROUPS
    grouped = updated.astype(jnp.float32).reshape(frames, tok_shard, GROUPS, group_width)
    sum_parts = jnp.sum(grouped, axis=(1, 3))
    square_parts = jnp.sum(grouped * grouped, axis=(1, 3))
    group_sum, group_square = lax.psum((sum_parts, square_parts), "row")
    counted = tok_shard * lax.axis_size("row") * group_width
    group_mean = group_sum / counted
    group_var = group_square / counted - group_mean * group_mean
    scaled = (grouped - group_mean[:, None, :, None]) * lax.rsqrt(group_var + 1e-05)[
        :, None, :, None
    ]
    activated = jax.nn.silu(
        scaled.reshape(frames, tok_shard, channels) * gn_gain.astype(jnp.float32)
    )
    activated = activated.astype(jnp.bfloat16).reshape(frames, row_count, col_count, channels)
    padded = with_halo(activated, (("row", 1),), 1)
    padded = jnp.pad(padded, ((0, 0), (0, 0), (1, 1), (0, 0)))
    convolved = jnp.zeros((frames * tok_shard, channels), jnp.float32)
    for row_off in range(3):
        for col_off in range(3):
            window = padded[
                :, row_off : row_off + row_count, col_off : col_off + col_count, :
            ].reshape(frames * tok_shard, channels)
            convolved = convolved + jnp.dot(
                window, conv_weight[row_off, col_off], preferred_element_type=jnp.float32
            )
    output = updated.astype(jnp.float32) + convolved + conv_bias.astype(jnp.float32)
    return output.astype(jnp.bfloat16).reshape(frames, row_count, col_count, channels)


def solution(mesh):
    in_specs = (P("frame", "row", None, None), P(), P(), P(), P(), P(), P(), P(), P())
    out_specs = P("frame", "row", None, None)
    return jax.shard_map(body, mesh=mesh, in_specs=in_specs, out_specs=out_specs, check_vma=False)
```

profile of v0, /device:TPU:1, one launch (start us, length us, event | category | flops | bytes accessed | tf_op | source)
XLA Modules:
  0.0 901.8 jit_solution(13939154227271930684)
XLA Ops:
  6.5 1.2 convert_reduce_fusion
  7.8 1.3 multiply_reduce_fusion.1
  9.9 1.2 multiply_convert_fusion.1
  12.4 10.2 %all-to-all-start.1 = ((bf16[4,128,1,8,40]{1,4,0,2,3:T(8,128)(2,1)}), bf16[4,128,1,8,40]{1,4,0,2,3:T(8,128)(2,1)S(1)}, u32[]{:S(2)}, u32[]{:S(2)}) async-start(bf16[4,128,1,8,40]{1,4,0,2,3:T(8,128)(2,1)} %copy.107), calls=%async_computation.1 | async-start | bytes 655360 | tf_op jit(solution)/shard_map/all_to_all | solution.py:87
  23.2 1.8 collective-permute-start
  26.3 2.2 collective-permute-done
  29.0 741.8 %all-reduce.4.cloned.1.call-done = bf16[1,128,2,8,40]{1,4,3,2,0:T(8,128)(2,1)} async-done(((bf16[1,128,2,8,40]{1,4,3,2,0:T(8,128)(2,1)}), bf16[1,128,2,8,40]{1,4,3,2,0:T(8,128)(2,1)}) %all-reduce.4.cloned.1.call-update) | async-done | bytes 163856 | tf_op jit(solution)/shard_map/psum | solution.py:13
  774.1 27.1 %all-to-all-start = ((bf16[5,128,2,8,40]{1,4,2,0,3:T(8,128)(2,1)}), bf16[5,128,2,8,40]{1,4,2,0,3:T(8,128)(2,1)S(1)}, u32[]{:S(2)}, u32[]{:S(2)}) async-start(bf16[5,128,2,8,40]{1,4,2,0,3:T(8,128)(2,1)} %copy.105), calls=%async_computation | async-start | bytes 1638400 | tf_op jit(solution)/shard_map/all_to_all | solution.py:88
  801.5 20.5 %all-to-all-done = bf16[5,128,2,8,40]{1,4,2,0,3:T(8,128)(2,1)S(1)} async-done(((bf16[5,128,2,8,40]{1,4,2,0,3:T(8,128)(2,1)}), bf16[5,128,2,8,40]{1,4,2,0,3:T(8,128)(2,1)S(1)}, u32[]{:S(2)}, u32[]{:S(2)}) %all-to-all-start) | async-done | bytes 819232 | tf_op jit(solution)/shard_map/all_to_all | solution.py:88
  822.2 19.6 %while.10 = (s32[]{:T(128)}, bf16[4,1024,1,40]{1,3,2,0:T(8,128)(2,1)S(1)}, bf16[4,1024,1,40]{1,3,2,0:T(8,128)(2,1)S(1)}, bf16[1024,1,40]{0,2,1:T(8,128)(2,1)S(1)...) while((s32[]{:T(128)}, ...), condition=%wide.region_6.7_spmd, body=%wide.region_3.6_spmd.sunk | while | flops 353056768 | bytes 26005600 | solution.py:65
  822.3 1.4 multiply_reduce_fusion.4
  823.6 1.9 fusion.91
  825.6 1.5 fusion.92
  827.2 1.4 multiply_reduce_fusion.4
  828.5 1.9 fusion.91
  830.5 1.5 fusion.92
  832.1 1.4 multiply_reduce_fusion.4
  833.4 1.9 fusion.91
  835.4 1.5 fusion.92
  837.0 1.4 multiply_reduce_fusion.4
  838.3 1.9 fusion.91
  840.3 1.5 fusion.92
  842.6 2.3 reshape.146
  844.9 4.2 all-to-all-start.2
  849.3 9.8 %all-to-all-done.2 = bf16[8,2,10240]{2,1,0:T(2,128)(2,1)S(1)} async-done(((bf16[8,2,10240]{2,1,0:T(2,128)(2,1)}), bf16[8,2,10240]{2,1,0:T(2,128)(2,1)S(1)}, u32[]{:S(2)}, u32[]{:S(2)}) %all-to-all-start.2) | async-done | bytes 327712 | tf_op jit(solution)/shard_map/all_to_all | solution.py:93
  859.1 1.6 reshape.147
  863.0 14.1 %all-reduce.1 = (f32[4,32]{1,0:T(4,128)S(1)}, f32[4,32]{1,0:T(4,128)S(1)}) all-reduce(f32[4,32]{1,0:T(4,128)S(1)} %copy.116, f32[4,32]{1,0:T(4,128)S(1)} %copy.115), channel_id=1, replica_groups=mesh['frame'=64,'row'=8] {'row'}, use_global_device_ids=true, to_apply=%region_10.11 | all-reduce | flops 256 | bytes 2048 | tf_op jit(solution)/shard_map/psum | solution.py:101
  878.4 1.9 collective-permute-start.1
  880.3 2.8 collective-permute-start.2
  883.8 2.7 collective-permute-done.2
  886.6 1.2 fusion.41
  888.2 1.2 copy-done.2
  (84 shorter events, 19.2 us)
Async XLA Ops:
  6.5 4.6 copy-start
  6.5 16.1 %copy-start.7 = (bf16[320,320]{1,0:T(8,128)(2,1)S(1)}, bf16[320,320]{1,0:T(8,128)(2,1)}, u32[]{:S(2)}) copy-start(bf16[320,320]{1,0:T(8,128)(2,1)} %param.14) | copy-start | bytes 614404
  6.5 16.1 %copy-start.6 = (bf16[320,320]{1,0:T(8,128)(2,1)S(1)}, bf16[320,320]{1,0:T(8,128)(2,1)}, u32[]{:S(2)}) copy-start(bf16[320,320]{1,0:T(8,128)(2,1)} %param.15) | copy-start | bytes 614404
  12.4 761.8 %all-to-all-start.1 = ((bf16[4,128,1,8,40]{1,4,0,2,3:T(8,128)(2,1)}), bf16[4,128,1,8,40]{1,4,0,2,3:T(8,128)(2,1)S(1)}, u32[]{:S(2)}, u32[]{:S(2)}) async-start(bf16[4,128,1,8,40]{1,4,0,2,3:T(8,128)(2,1)} %copy.107), calls=%async_computation.1 | async-start | bytes 655360 | tf_op jit(solution)/shard_map/all_to_all | solution.py:87
  22.6 748.3 %all-reduce.4.cloned.1.call-start = ((), (), s32[]{:S(2)}) async-start(), calls=%async_computation.3 | async-start | bytes 327680 | tf_op jit(solution)/shard_map/psum | solution.py:13
  23.2 5.3 collective-permute-start
  774.1 47.9 %all-to-all-start = ((bf16[5,128,2,8,40]{1,4,2,0,3:T(8,128)(2,1)}), bf16[5,128,2,8,40]{1,4,2,0,3:T(8,128)(2,1)S(1)}, u32[]{:S(2)}, u32[]{:S(2)}) async-start(bf16[5,128,2,8,40]{1,4,2,0,3:T(8,128)(2,1)} %copy.105), calls=%async_computation | async-start | bytes 1638400 | tf_op jit(solution)/shard_map/all_to_all | solution.py:88
  841.8 7.2 copy-start.1
  841.8 7.4 copy-start.4
  844.9 14.2 %all-to-all-start.2 = ((bf16[8,2,10240]{2,1,0:T(2,128)(2,1)}), bf16[8,2,10240]{2,1,0:T(2,128)(2,1)S(1)}, u32[]{:S(2)}, u32[]{:S(2)}) async-start(bf16[8,2,10240]{2,1,0:T(2,128)(2,1)} %reshape.146), calls=%async_computation.2 | async-start | bytes 655360 | tf_op jit(solution)/shard_map/all_to_all | solution.py:93
  849.1 12.6 %copy-start.3 = (bf16[320,320]{1,0:T(8,128)(2,1)S(1)}, bf16[320,320]{1,0:T(8,128)(2,1)}, u32[]{:S(2)}) copy-start(bf16[320,320]{1,0:T(8,128)(2,1)} %param.16) | copy-start | bytes 614404
  862.2 20.9 %copy-start.5 = (bf16[320]{0:T(512)(128)(2,1)S(1)}, bf16[320]{0:T(512)(128)(2,1)}, u32[]{:S(2)}) copy-start(bf16[320]{0:T(512)(128)(2,1)} %param.19) | copy-start | bytes 1924
  878.4 5.4 collective-permute-start.1
  880.3 6.3 collective-permute-start.2
  887.8 1.6 copy-start.2
Sparse Core Ops, SparseCore 0:
  26.3 744.4 all-reduce.3
where the time goes:
time: 902 us
  waiting for transfers between devices  777 us (86%)
  starting transfers between devices  48 us (5%)
  matrix products  16.6 us (2%)
  other arithmetic  16.1 us (2%)
  local copies, waits for them, and re-layouts  15.9 us (2%)
  blocking collectives  14.1 us (2%)
  between operations  13.9 us (2%)
    psum x1, waiting for transfers between devices, spread_2(): return lax.psum(kept, axis)  742 us
    all_to_all x1, starting transfers between devices, body(): lax.all_to_all(sent_pairs, 'row', split_axis=3, concat_axis=1, tiled=True)  27.1 us
    all_to_all x1, waiting for transfers between devices, body(): lax.all_to_all(sent_pairs, 'row', split_axis=3, concat_axis=1, tiled=True)  20.5 us
  transfers between devices with their start and end apart: 7, of which 5 were waited for; matrix products, arithmetic and copies ran while one was open for 1% of the time, Pallas kernels for 0%

commit v1 on v0

--- a/solution.py
+++ b/solution.py
@@ -10,7 +10,10 @@
 
 def spread_2(value, axis, source):
     kept = jnp.where(lax.axis_index(axis) == source, value, 0).astype(value.dtype)
-    return lax.psum(kept, axis)
+    draw_figure = lambda group_axis, work_x: jax.lax.all_gather(work_x, axis_name=group_axis).sum(
+        axis=0
+    )
+    return draw_figure(axis, kept)
 
 
 def shifted(block, axis, distance):

time: 902 us -> 359 us (0.40)
  waiting for transfers between devices: 777 us -> 250 us
  starting transfers between devices: 48 us -> 25.7 us
    psum x1 -> x0, waiting for transfers between devices: 742 us -> none  [spread_2(): return lax.psum(kept, axis)]
    all_gather x0 -> x1, waiting for transfers between devices: none -> 214 us  [spread_2(): jax.lax.all_gather(work_x, axis_name=group_axis).sum(axis=0)]
    all_to_all x1, starting transfers between devices: 27.1 us -> 4.6 us  [body(): lax.all_to_all(sent_pairs, 'row', split_axis=3, concat_axis=1, tiled=True)]
  transfers between devices with their start and end apart: 7 -> 7, of which waited for: 5 -> 5; matrix products, arithmetic and copies ran while one was open for 1% -> 3% of each run, Pallas kernels for 0% -> 0%
where the time goes in v1:
time: 359 us; the launch traced here: 358 us
  waiting for transfers between devices  250 us (70%)
  starting transfers between devices  25.7 us (7%)
  other arithmetic  22.5 us (6%)
  matrix products  17.6 us (5%)
  local copies, waits for them, and re-layouts  14.4 us (4%)
  blocking collectives  14.1 us (4%)
  between operations  13.8 us (4%)
    all_gather x1, waiting for transfers between devices, spread_2(): jax.lax.all_gather(work_x, axis_name=group_axis).sum(axis=0)  214 us
    all_to_all x1, waiting for transfers between devices, body(): lax.all_to_all(sent_pairs, 'row', split_axis=3, concat_axis=1, tiled=True)  20.6 us
    psum x1, blocking collectives, body(): group_sum, group_square = lax.psum((sum_parts, square_parts), 'row')  14.1 us
    all_to_all x1, starting transfers between devices, body(): lax.all_to_all(sent_queries, 'row', split_axis=3, concat_axis=1, tiled=True)  10.2 us
    all_to_all x1, waiting for transfers between devices, body(): lax.all_to_all(head_results, 'row', split_axis=1, concat_axis=2, tiled=True)  9.84 us
    reduce_sum x4, other arithmetic, single(): totals = jnp.sum(raised, axis=-1)  7.73 us
  transfers between devices with their start and end apart: 7, of which 5 were waited for; matrix products, arithmetic and copies ran while one was open for 3% of the time, Pallas kernels for 0%

profile of v1, /device:TPU:1, one launch (start us, length us, event | category | flops | bytes accessed | tf_op | source)
XLA Modules:
  0.0 358.4 jit_solution(12490510962905152881)
XLA Ops:
  7.7 1.3 multiply_reduce_fusion.1
  11.1 1.6 convolution_convert_fusion
  14.7 10.2 %all-to-all-start.1 = ((bf16[4,128,1,8,40]{1,4,0,2,3:T(8,128)(2,1)}), bf16[4,128,1,8,40]{1,4,0,2,3:T(8,128)(2,1)S(1)}, u32[]{:S(2)}, u32[]{:S(2)}) async-start(bf16[4,128,1,8,40]{1,4,0,2,3:T(8,128)(2,1)} %copy.105), calls=%async_computation.1 | async-start | bytes 655360 | tf_op jit(solution)/shard_map/all_to_all | solution.py:90
  24.9 1.7 collective-permute-start
  27.2 3.1 collective-permute-done
  30.8 214.0 %all-gather.3.cloned.1.call-done = bf16[8192,640]{1,0:T(8,128)(2,1)} async-done(((bf16[128,640]{1,0:T(8,128)(2,1)}), bf16[8192,640]{1,0:T(8,128)(2,1)}) %all-gather.3.cloned.1.call-update) | async-done | bytes 10485776 | tf_op jit(solution)/shard_map/all_gather | solution.py:13
  244.8 5.8 %reduce_sum.59 = bf16[128,640]{1,0:T(8,128)(2,1)S(1)} reduce(bf16[64,128,640]{2,1,0:T(8,128)(2,1)} %bitcast.143, bf16[]{:T(256)} %constant.37.clone.1), dimensions={0}, to_apply=%region_2.3 | reduce | flops 5160960 | bytes 10649602 | tf_op jit(solution)/shard_map/reduce_sum | solution.py:13
  253.1 4.6 %all-to-all-start = ((bf16[5,128,2,8,40]{1,4,2,0,3:T(8,128)(2,1)}), bf16[5,128,2,8,40]{1,4,2,0,3:T(8,128)(2,1)S(1)}, u32[]{:S(2)}, u32[]{:S(2)}) async-start(bf16[5,128,2,8,40]{1,4,2,0,3:T(8,128)(2,1)} %copy.103), calls=%async_computation | async-start | bytes 1638400 | tf_op jit(solution)/shard_map/all_to_all | solution.py:91
  258.0 20.6 %all-to-all-done = bf16[5,128,2,8,40]{1,4,2,0,3:T(8,128)(2,1)S(1)} async-done(((bf16[5,128,2,8,40]{1,4,2,0,3:T(8,128)(2,1)}), bf16[5,128,2,8,40]{1,4,2,0,3:T(8,128)(2,1)S(1)}, u32[]{:S(2)}, u32[]{:S(2)}) %all-to-all-start) | async-done | bytes 819232 | tf_op jit(solution)/shard_map/all_to_all | solution.py:91
  278.7 19.6 %while.10 = (s32[]{:T(128)}, bf16[4,1024,1,40]{1,3,2,0:T(8,128)(2,1)S(1)}, bf16[4,1024,1,40]{1,3,2,0:T(8,128)(2,1)S(1)}, bf16[1024,1,40]{0,2,1:T(8,128)(2,1)S(1)...) while((s32[]{:T(128)}, ...), condition=%wide.region_6.7_spmd, body=%wide.region_3.6_spmd.sunk | while | flops 353056768 | bytes 26005600 | solution.py:68
  278.8 1.4 multiply_reduce_fusion.4
  280.1 1.9 fusion.91
  282.1 1.5 fusion.92
  283.7 1.4 multiply_reduce_fusion.4
  285.0 1.9 fusion.91
  287.0 1.5 fusion.92
  288.5 1.4 multiply_reduce_fusion.4
  289.9 1.9 fusion.91
  291.9 1.5 fusion.92
  293.4 1.4 multiply_reduce_fusion.4
  294.8 1.9 fusion.91
  296.7 1.5 fusion.92
  299.1 2.3 reshape.147
  301.3 4.2 %all-to-all-start.2 = ((bf16[8,2,10240]{2,1,0:T(2,128)(2,1)}), bf16[8,2,10240]{2,1,0:T(2,128)(2,1)S(1)}, u32[]{:S(2)}, u32[]{:S(2)}) async-start(bf16[8,2,10240]{2,1,0:T(2,128)(2,1)} %reshape.147), calls=%async_computation.2 | async-start | bytes 655360 | tf_op jit(solution)/shard_map/all_to_all | solution.py:96
  305.8 9.8 %all-to-all-done.2 = bf16[8,2,10240]{2,1,0:T(2,128)(2,1)S(1)} async-done(((bf16[8,2,10240]{2,1,0:T(2,128)(2,1)}), bf16[8,2,10240]{2,1,0:T(2,128)(2,1)S(1)}, u32[]{:S(2)}, u32[]{:S(2)}) %all-to-all-start.2) | async-done | bytes 327712 | tf_op jit(solution)/shard_map/all_to_all | solution.py:96
  315.6 1.6 reshape.148
  319.5 14.1 %all-reduce.1 = (f32[4,32]{1,0:T(4,128)S(1)}, f32[4,32]{1,0:T(4,128)S(1)}) all-reduce(f32[4,32]{1,0:T(4,128)S(1)} %copy.114, f32[4,32]{1,0:T(4,128)S(1)} %copy.113), channel_id=1, replica_groups=mesh['frame'=64,'row'=8] {'row'}, use_global_device_ids=true, to_apply=%region_10.11 | all-reduce | flops 256 | bytes 2048 | tf_op jit(solution)/shard_map/psum | solution.py:104
  334.9 1.9 collective-permute-start.1
  336.8 3.1 collective-permute-start.2
  340.5 2.5 collective-permute-done.2
  343.1 1.2 fusion.41
  344.7 1.2 copy-done.2
  (81 shorter events, 20.1 us)
Async XLA Ops:
  6.5 6.9 %copy-start = (bf16[320,320]{1,0:T(8,128)(2,1)S(1)}, bf16[320,320]{1,0:T(8,128)(2,1)}, u32[]{:S(2)}) copy-start(bf16[320,320]{1,0:T(8,128)(2,1)} %param.13) | copy-start | bytes 614404
  6.5 238.2 %all-gather.3.cloned.1.call-start = ((), (), s32[]{:S(2)}) async-start(), calls=%async_computation.3 | async-start | bytes 10649600 | tf_op jit(solution)/shard_map/all_gather | solution.py:13
  14.7 238.4 %all-to-all-start.1 = ((bf16[4,128,1,8,40]{1,4,0,2,3:T(8,128)(2,1)}), bf16[4,128,1,8,40]{1,4,0,2,3:T(8,128)(2,1)S(1)}, u32[]{:S(2)}, u32[]{:S(2)}) async-start(bf16[4,128,1,8,40]{1,4,0,2,3:T(8,128)(2,1)} %copy.105), calls=%async_computation.1 | async-start | bytes 655360 | tf_op jit(solution)/shard_map/all_to_all | solution.py:90
  24.9 5.4 %collective-permute-start = (bf16[128,640]{1,0:T(8,128)(2,1)S(1)}, bf16[128,640]{1,0:T(8,128)(2,1)S(1)}, u32[]{:S(2)}, u32[]{:S(2)}) collective-permute-start(bf16[128,640]{1,0:T(8,128)(2,1)S(1)} %get-tuple-element.118), channel_id=1, source_target_pairs={{0,8},{8,16},{16,24},{24,32},{32,40},{40,48},{48,56},{56,64},{64,7... | collective-permute-start | bytes 491528 | tf_op jit(solution)/shard_map/ppermute | solution.py:22
  253.1 25.4 %all-to-all-start = ((bf16[5,128,2,8,40]{1,4,2,0,3:T(8,128)(2,1)}), bf16[5,128,2,8,40]{1,4,2,0,3:T(8,128)(2,1)S(1)}, u32[]{:S(2)}, u32[]{:S(2)}) async-start(bf16[5,128,2,8,40]{1,4,2,0,3:T(8,128)(2,1)} %copy.103), calls=%async_computation | async-start | bytes 1638400 | tf_op jit(solution)/shard_map/all_to_all | solution.py:91
  298.3 7.3 %copy-start.1 = (bf16[4,4,32,320]{3,2,1,0:T(8,128)(2,1)S(1)}, bf16[4,4,32,320]{3,2,1,0:T(8,128)(2,1)}, u32[]{:S(2)}) copy-start(bf16[4,4,32,320]{3,2,1,0:T(8,128)(2,1)} %param.11) | copy-start | bytes 983044
  298.3 7.4 %copy-start.4 = (bf16[320]{0:T(512)(128)(2,1)S(1)}, bf16[320]{0:T(512)(128)(2,1)}, u32[]{:S(2)}) copy-start(bf16[320]{0:T(512)(128)(2,1)} %param.17) | copy-start | bytes 1924
  301.3 14.3 %all-to-all-start.2 = ((bf16[8,2,10240]{2,1,0:T(2,128)(2,1)}), bf16[8,2,10240]{2,1,0:T(2,128)(2,1)S(1)}, u32[]{:S(2)}, u32[]{:S(2)}) async-start(bf16[8,2,10240]{2,1,0:T(2,128)(2,1)} %reshape.147), calls=%async_computation.2 | async-start | bytes 655360 | tf_op jit(solution)/shard_map/all_to_all | solution.py:96
  305.6 12.6 %copy-start.3 = (bf16[320,320]{1,0:T(8,128)(2,1)S(1)}, bf16[320,320]{1,0:T(8,128)(2,1)}, u32[]{:S(2)}) copy-start(bf16[320,320]{1,0:T(8,128)(2,1)} %param.16) | copy-start | bytes 614404
  318.7 21.1 %copy-start.5 = (bf16[320]{0:T(512)(128)(2,1)S(1)}, bf16[320]{0:T(512)(128)(2,1)}, u32[]{:S(2)}) copy-start(bf16[320]{0:T(512)(128)(2,1)} %param.19) | copy-start | bytes 1924
  334.9 5.6 %collective-permute-start.1 = (bf16[4,1,32,320]{3,2,1,0:T(8,128)(2,1)}, bf16[4,1,32,320]{3,2,1,0:T(8,128)(2,1)S(1)}, u32[]{:S(2)}, u32[]{:S(2)}) collective-permute-start(bf16[4,1,32,320]{3,2,1,0:T(8,128)(2,1)} %get-tuple-element.121), channel_id=1, source_target_pairs={{0,1},{1,2},{2,3},{3,4},{4,5},{5,6},{6,7},{8,9},{9,10},{10,11},{11... | collective-permute-start | bytes 245768 | tf_op jit(solution)/shard_map/ppermute | solution.py:32
  336.8 6.3 %collective-permute-start.2 = (bf16[4,1,32,320]{3,2,1,0:T(8,128)(2,1)}, bf16[4,1,32,320]{3,2,1,0:T(8,128)(2,1)}, u32[]{:S(2)}, u32[]{:S(2)}) collective-permute-start(bf16[4,1,32,320]{3,2,1,0:T(8,128)(2,1)} %get-tuple-element.122), channel_id=1, source_target_pairs={{1,0},{2,1},{3,2},{4,3},{5,4},{6,5},{7,6},{9,8},{10,9},{11,10},{12... | collective-permute-start | bytes 245768 | tf_op jit(solution)/shard_map/ppermute | solution.py:33
  344.3 1.6 copy-start.2
Sparse Core Ops, SparseCore 0:
  13.6 231.1 all-gather.2
